TPU v7x, 256 devices: a whole 4x4x8 slice. The times are simulated.
256 devices in a mesh: ctx: 16 (over z, core), exp: 16 (over x, y).
Axes of the slice: x: 4, y: 4, z: 8, core: 2. Of those that a mesh axis runs over, the one named last changes fastest.
Arguments:
- query_input: bfloat16 [2048, 8192], P('ctx', 'exp'), may hold values from -6 to 6
- key_input: bfloat16 [2048, 8192], P('ctx', 'exp'), may hold values from -6 to 6
- value_input: bfloat16 [2048, 8192], P('ctx', 'exp'), may hold values from -6 to 6
- gate_logits: float32 [2, 2048, 64], P(None, 'ctx', 'exp'), may hold values from -6 to 6
- comp_weight: float32 [2, 32, 64], P(None, None, 'exp'), may hold values from -6 to 6
- out_proj: bfloat16 [8192, 7168], P('exp', 'ctx'), may hold values from -0.0625 to 0.0625
- residual_in: bfloat16 [2048, 7168], P(('ctx', 'exp')), may hold values from -3 to 3
- ffn_gain: float32 [7168], replicated, may hold values from 0.25 to 1.75
- expert_ids: int32 [2048, 2], P(('ctx', 'exp')), may hold values from 0 to 15, all different within a row; in each aligned block of 8 rows (0 to 7, 8 to 15, ...) at most 2 rows name the same one
- route_gates: float32 [2048, 2], P(('ctx', 'exp')), may hold values from 0.2 to 1
- expert_gate: bfloat16 [16, 7168, 2048], P('exp', None, 'ctx'), may hold values from -0.0625 to 0.0625
- expert_up: bfloat16 [16, 7168, 2048], P('exp', None, 'ctx'), may hold values from -0.0625 to 0.0625
- expert_down: bfloat16 [16, 2048, 7168], P('exp', 'ctx'), may hold values from -0.125 to 0.125
Outputs:
- layer_out: bfloat16 [2048, 7168], P(('ctx', 'exp'))
Inputs may be any that keep to these rules, and one draw needn't show every extreme that they name: `expert_ids`: each token names 2 different experts. In every aligned block of 8 consecutive tokens no expert is named more than 2 times, a bound that some block reaches.
All inputs are finite; a program needn't handle non-finite values.
Results may differ from a plain program's by a relative error of at most 0.0085.
Values may be sent and summed in bfloat16 or wider, within the bound.
A program may use at most 128 MiB of HBM per device.

v0:
```python
import math
import jax
import jax.numpy as jnp
from jax import lax
from jax.sharding import PartitionSpec as P

WINDOW = 512
score_gain = 2.0
norm_eps = 1e-06


def passed_along(block, axis, distance):
    devices = range(lax.axis_size(axis))
    route = [(i - distance, i) for i in devices if i - distance in devices]
    return lax.ppermute(block, axis, route)


def head_norm(matrix, head_width):
    row_count = matrix.shape[0]
    shaped = matrix.reshape(row_count, -1, head_width).astype(jnp.float32)
    scaled = shaped * lax.rsqrt(jnp.mean(shaped * shaped, axis=2, keepdims=True) + norm_eps)
    return scaled.reshape(row_count, -1)


def compress(extended, position_weights, head_width):
    stride_len = position_weights.shape[0] // 2
    head_count = position_weights.shape[1]
    blocks = extended.reshape(-1, stride_len, head_count, head_width).astype(jnp.float32)
    first_half = jnp.einsum(
        "nshd,sh->nhd", blocks[:-1], position_weights[:stride_len], precision=lax.Precision.HIGHEST
    )
    second_half = jnp.einsum(
        "nshd,sh->nhd", blocks[1:], position_weights[stride_len:], precision=lax.Precision.HIGHEST
    )
    return (first_half + second_half).reshape(blocks.shape[0] - 1, head_count * head_width)


def local(
    query_input,
    key_input,
    value_input,
    gate_logits,
    comp_weight,
    out_proj,
    residual_in,
    ffn_gain,
    expert_ids,
    route_gates,
    expert_gate,
    expert_up,
    expert_down,
):
    row_count = query_input.shape[0]
    head_count = comp_weight.shape[2]
    head_width = query_input.shape[1] // head_count
    block_len = comp_weight.shape[1]
    stride_len = block_len // 2
    exp_count = lax.axis_size("exp")
    ctx_index = lax.axis_index("ctx")
    scale = score_gain / math.sqrt(head_width)
    query_norm = head_norm(query_input, head_width).astype(jnp.bfloat16)
    key_norm = head_norm(key_input, head_width).astype(jnp.bfloat16)
    next_keys, next_values = passed_along(
        (key_input[:stride_len], value_input[:stride_len]), "ctx", -1
    )
    comp_keys = head_norm(
        compress(jnp.concatenate([key_input, next_keys], 0), comp_weight[0], head_width), head_width
    ).astype(jnp.bfloat16)
    comp_values = compress(
        jnp.concatenate([value_input, next_values], 0), comp_weight[1], head_width
    ).astype(jnp.bfloat16)
    query_pos = ctx_index * row_count + jnp.arange(row_count, dtype=jnp.int32)
    query_heads = query_norm.reshape(row_count, head_count, head_width)
    part_keys = lax.all_gather(comp_keys, "ctx", axis=0, tiled=True)
    part_values = lax.all_gather(comp_values, "ctx", axis=0, tiled=True)
    part_count = part_keys.shape[0]
    scores = jnp.einsum(
        "thd,nhd->htn",
        query_heads,
        part_keys.reshape(part_count, head_count, head_width),
        preferred_element_type=jnp.float32,
    )
    block_end = jnp.arange(part_count, dtype=jnp.int32) * stride_len + block_len - 1
    visible = block_end[None, :] <= query_pos[:, None]
    weights = jnp.where(visible[None], jnp.exp(scale * scores), 0.0)
    running_total = jnp.sum(weights, axis=2).T
    collected = jnp.einsum(
        "htn,nhd->thd",
        weights.astype(jnp.bfloat16),
        part_values.reshape(part_count, head_count, head_width),
        preferred_element_type=jnp.float32,
    )
    cmp_sum = collected.reshape(row_count, -1)
    no_block = (query_pos < block_len - 1).astype(jnp.float32)
    cmp_out = (
        cmp_sum.reshape(row_count, head_count, head_width)
        / (running_total + no_block[:, None])[:, :, None]
    )
    shift_count = max(1, WINDOW // row_count)
    earlier_keys = []
    earlier_values = []
    for distance in range(shift_count, 0, -1):
        moved_keys, moved_values = passed_along((key_norm, value_input), "ctx", distance)
        earlier_keys.append(moved_keys)
        earlier_values.append(moved_values)
    near_keys = jnp.concatenate(earlier_keys + [key_norm], 0)
    near_values = jnp.concatenate(earlier_values + [value_input], 0)
    key_pos = ctx_index * row_count - WINDOW + jnp.arange(near_keys.shape[0], dtype=jnp.int32)
    near_scores = jnp.einsum(
        "thd,shd->hts",
        query_heads,
        near_keys.reshape(-1, head_count, head_width),
        preferred_element_type=jnp.float32,
    )
    inside = (
        (key_pos[None, :] <= query_pos[:, None])
        & (key_pos[None, :] > query_pos[:, None] - WINDOW)
        & (key_pos[None, :] >= 0)
    )
    near_weights = jnp.where(inside[None], jnp.exp(scale * near_scores), 0.0)
    win_total = jnp.sum(near_weights, axis=2).T
    win_sum = jnp.einsum(
        "hts,shd->thd",
        near_weights.astype(jnp.bfloat16),
        near_values.reshape(-1, head_count, head_width),
        preferred_element_type=jnp.float32,
    )
    win_out = win_sum / win_total[:, :, None]
    branch_gates = jax.nn.sigmoid(gate_logits)
    attended = (
        (branch_gates[0][:, :, None] * cmp_out + branch_gates[1][:, :, None] * win_out)
        .reshape(row_count, -1)
        .astype(jnp.bfloat16)
    )
    token_share = row_count // exp_count
    partial_sum = jnp.dot(
        attended,
        lax.all_gather(out_proj, "ctx", axis=1, tiled=True),
        preferred_element_type=jnp.float32,
    )
    projected = lax.psum_scatter(partial_sum, "exp", scatter_dimension=0, tiled=True)
    hidden_state = residual_in.astype(jnp.float32) + projected
    mean_square = jnp.mean(hidden_state * hidden_state, axis=1, keepdims=True)
    normed = (hidden_state * lax.rsqrt(mean_square + norm_eps) * ffn_gain).astype(jnp.bfloat16)
    model_width = normed.shape[1]
    top_count = expert_ids.shape[1]
    capacity = max(2, 2 * token_share * top_count // exp_count)
    flat_ids = expert_ids.reshape(-1)
    chosen = (flat_ids[:, None] == jnp.arange(exp_count, dtype=jnp.int32)[None, :]).astype(
        jnp.int32
    )
    slots = jnp.sum((jnp.cumsum(chosen, axis=0) - chosen) * chosen, axis=1)
    targets = (flat_ids * capacity + slots).reshape(token_share, top_count)
    slot_range = jnp.arange(exp_count * capacity, dtype=jnp.int32)
    dispatch_map = jnp.sum(
        (slot_range[:, None, None] == targets[None, :, :]).astype(jnp.float32), axis=2
    ).astype(jnp.bfloat16)
    outgoing = (
        jnp.dot(dispatch_map, normed, preferred_element_type=jnp.float32)
        .astype(jnp.bfloat16)
        .reshape(exp_count, capacity, model_width)
    )
    arrived = lax.all_to_all(outgoing, "exp", split_axis=0, concat_axis=0, tiled=True)
    gate_cols = expert_gate[0]
    up_cols = expert_up[0]
    down_rows = expert_down[0]
    portion = lax.all_gather(arrived, "ctx", axis=0, tiled=True)
    flat_rows = portion.reshape(-1, model_width)
    gate_part = jnp.dot(flat_rows, gate_cols, preferred_element_type=jnp.float32)
    up_part = jnp.dot(flat_rows, up_cols, preferred_element_type=jnp.float32)
    activated = (jax.nn.silu(gate_part) * up_part).astype(jnp.bfloat16)
    partial_out = jnp.dot(activated, down_rows, preferred_element_type=jnp.float32).reshape(
        portion.shape
    )
    finished = lax.psum_scatter(
        partial_out.astype(jnp.bfloat16), "ctx", scatter_dimension=0, tiled=True
    )
    returned = lax.all_to_all(finished, "exp", split_axis=0, concat_axis=0, tiled=True).reshape(
        -1, model_width
    )
    combine_map = jnp.sum(
        jnp.where(slot_range[None, None, :] == targets[:, :, None], route_gates[:, :, None], 0.0),
        axis=1,
    )
    moe_out = jnp.dot(combine_map, returned.astype(jnp.float32), precision=lax.Precision.HIGHEST)
    return (hidden_state + moe_out).astype(jnp.bfloat16)


def solution(mesh):
    in_specs = (
        P("ctx", "exp"),
        P("ctx", "exp"),
        P("ctx", "exp"),
        P(None, "ctx", "exp"),
        P(None, None, "exp"),
        P("exp", "ctx"),
        P(("ctx", "exp"), None),
        P(),
        P(("ctx", "exp"), None),
        P(("ctx", "exp"), None),
        P("exp", None, "ctx"),
        P("exp", None, "ctx"),
        P("exp", "ctx", None),
    )
    out_specs = P(("ctx", "exp"), None)
    return jax.shard_map(local, mesh=mesh, in_specs=in_specs, out_specs=out_specs, check_vma=False)
```

profile of v0, /device:TPU:8, one launch (start us, length us, event | category | flops | bytes accessed | tf_op | source)
XLA Modules:
  0.0 412.8 jit_solution(15140837322775450915)
XLA Ops:
  6.6 0.7 all-gather.3.cloned.1.call-update
  7.3 1.0 copy.91
  8.4 5.2 %collective-permute-start.6 = (bf16[128,512]{0,1:T(8,128)(2,1)S(1)}, bf16[128,512]{0,1:T(8,128)(2,1)S(1)}, u32[]{:S(2)}, u32[]{:S(2)}) collective-permute-start(bf16[128,512]{0,1:T(8,128)(2,1)S(1)} %fusion.24), channel_id=1, source_target_pairs={{0,64},{16,80},{32,96},{48,112},{64,128},{80,144},{96,160},{112,17... | collective-permute-start | bytes 393224 | tf_op jit(solution)/shard_map/ppermute | solution.py:15
  13.6 3.0 collective-permute-start.7
  16.6 5.0 %collective-permute-start.8 = (bf16[128,512]{0,1:T(8,128)(2,1)S(1)}, bf16[128,512]{0,1:T(8,128)(2,1)S(1)}, u32[]{:S(2)}, u32[]{:S(2)}) collective-permute-start(bf16[128,512]{0,1:T(8,128)(2,1)S(1)} %fusion.24), channel_id=1, source_target_pairs={{0,32},{16,48},{32,64},{48,80},{64,96},{80,112},{96,128},{112,144}... | collective-permute-start | bytes 393224 | tf_op jit(solution)/shard_map/ppermute | solution.py:15
  21.7 3.4 collective-permute-start.2
  25.1 1.3 slice.74
  26.4 1.3 collective-permute-start.1
  27.7 1.6 slice.71
  29.3 0.9 slice.63
  30.2 0.9 convert_multiply_fusion.3
  31.3 0.2 reduce_sum.83
  31.5 0.7 add_divide_fusion
  32.2 0.6 slice_bitcast_fusion.1
  32.8 1.4 fusion.49
  34.3 0.8 and_and_fusion
  35.1 1.1 fusion.30
  36.3 0.8 fusion.34
  37.1 0.2 mul.134
  37.3 0.7 slice.66
  38.0 3.6 collective-permute-start.3
  41.7 0.2 fusion.28
  42.1 18.2 %all_gather.13 = bf16[128,512]{1,0:T(8,128)(2,1)S(1)} all-gather(bf16[8,512]{1,0:T(8,128)(2,1)S(1)} %fusion.45), channel_id=1, replica_groups=mesh['ctx'=16,'exp'=16] {'ctx'}, dimensions={0}, use_global_device_ids=true | all-gather | bytes 139264 | tf_op jit(solution)/shard_map/all_gather | solution.py:74
  60.3 0.1 copy.86
  60.4 0.9 fusion.51
  61.3 2.9 collective-permute-start.4
  64.2 2.0 collective-permute-start.5
  66.2 4.5 %collective-permute-done.4 = bf16[128,512]{1,0:T(8,128)(2,1)S(1)} collective-permute-done((bf16[128,512]{1,0:T(8,128)(2,1)S(1)}, bf16[128,512]{1,0:T(8,128)(2,1)S(1)}, u32[]{:S(2)}, u32[]{:S(2)}) %collective-permute-start.4) | collective-permute-done | bytes 131104 | tf_op jit(solution)/shard_map/ppermute | solution.py:15
  70.8 1.9 collective-permute-start.9
  72.7 1.3 collective-permute-start
  74.1 4.0 collective-permute-done
  78.2 0.8 fusion.32
  79.0 0.7 fusion.44
  79.8 19.0 %all_gather.12 = bf16[128,512]{1,0:T(8,128)(2,1)S(1)} all-gather(bf16[8,512]{1,0:T(8,128)(2,1)S(1)} %fusion.44), channel_id=1, replica_groups=mesh['ctx'=16,'exp'=16] {'ctx'}, dimensions={0}, use_global_device_ids=true | all-gather | bytes 139264 | tf_op jit(solution)/shard_map/all_gather | solution.py:75
  98.9 0.3 copy.90
  99.2 0.1 copy.83
  99.3 0.7 constant_dynamic-update-slice_fusion.7
  100.0 1.6 constant_dynamic-update-slice_fusion.6
  101.6 0.7 constant_dynamic-update-slice_fusion.5
  102.3 1.7 fusion.50
  104.0 0.4 fusion.17
  104.4 0.2 fusion.18
  104.6 7.5 %fusion.52 = f32[128,7168]{1,0:T(8,128)} fusion(bf16[128,512]{0,1:T(8,128)(2,1)S(1)} %bitcast.126, bf16[512,7168]{0,1:T(8,128)(2,1)} %all-gather.3.cloned.1.call-done), kind=kOutput, calls=%fused_computation.101 | convolution fusion | flops 939524096 | bytes 11141120 | tf_op jit(solution)/shard_map/dot_general | solution.py:136
  112.2 0.6 copy-done.11
  113.1 0.2 select_reduce_fusion.1
  113.4 0.6 dynamic-slice
  114.8 107.4 %all-reduce.3.cloned.1.call-done = f32[128,7168]{1,0:T(8,128)} async-done(((f32[128,7168]{1,0:T(8,128)}), f32[128,7168]{1,0:T(8,128)}) %all-reduce.3.cloned.1.call-update) | async-done | bytes 3670032
  222.1 1.1 multiply_reduce_fusion
  223.3 1.3 convolution_convert_fusion.1
  224.6 0.2 reshape.231
  224.7 15.1 %all_to_all.10 = bf16[16,2,7168]{2,1,0:T(2,128)(2,1)} all-to-all(bf16[16,2,7168]{2,1,0:T(2,128)(2,1)S(1)} %reshape.231), channel_id=1, replica_groups=mesh['ctx'=16,'exp'=16] {'exp'}, dimensions={0} | all-to-all | bytes 917504 | tf_op jit(solution)/shard_map/all_to_all | solution.py:163
  239.8 0.2 reduce-scatter.2.cloned.1.call-start
  240.1 49.7 %all-gather.5.cloned.1.call-done = bf16[256,2,7168]{2,1,0:T(2,128)(2,1)} async-done(((bf16[16,2,7168]{2,1,0:T(2,128)(2,1)}), bf16[256,2,7168]{2,1,0:T(2,128)(2,1)}) %all-gather.5.cloned.1.call-update) | async-done | bytes 7340048 | tf_op jit(solution)/shard_map/all_gather | solution.py:167
  289.8 15.4 %reshape.232 = bf16[512,7168]{1,0:T(8,128)(2,1)} reshape(bf16[256,2,7168]{2,1,0:T(2,128)(2,1)} %all-gather.5.cloned.1.call-done) | data formatting | bytes 14680064 | tf_op jit(solution)/shard_map/reshape | solution.py:168
  305.2 5.8 %fusion.4 = f32[512,128]{1,0:T(8,128)S(1)} fusion(bf16[512,7168]{1,0:T(8,128)(2,1)} %reshape.232, bf16[1,7168,128]{2,1,0:T(8,128)(2,1)} %param.23), kind=kOutput, calls=%fused_computation.7 | convolution fusion | flops 939524096 | bytes 9437184 | tf_op jit(solution)/shard_map/dot_general | solution.py:169
  311.0 0.4 copy-done.13
  311.4 2.1 fusion.19
  313.4 5.0 %convolution_convert_fusion = bf16[256,2,7168]{2,0,1:T(8,128)(2,1)} fusion(bf16[1,128,7168]{2,1,0:T(8,128)(2,1)S(1)} %copy-done, bf16[256,2,128]{2,1,0:T(2,128)(2,1)S(1)} %bitcast.127), kind=kOutput, calls=%fused_computation | convolution fusion | flops 943194112 | bytes 9306112 | tf_op jit(solution)/shard_map/dot_general | solution.py:172
  318.5 67.8 %reduce-scatter.2.cloned.1.call-done = bf16[16,2,7168]{2,0,1:T(8,128)(2,1)} async-done(((bf16[256,2,7168]{2,0,1:T(8,128)(2,1)}), bf16[16,2,7168]{2,0,1:T(8,128)(2,1)}) %reduce-scatter.2.cloned.1.call-update) | async-done | bytes 458768 | tf_op jit(solution)/shard_map/reduce_scatter | solution.py:175
  386.3 2.3 copy.99
  388.6 7.3 %all-to-all-start.1 = ((bf16[16,2,7168]{2,1,0:T(2,128)(2,1)}), bf16[16,2,7168]{2,1,0:T(2,128)(2,1)S(1)}, u32[]{:S(2)}, u32[]{:S(2)}) async-start(bf16[16,2,7168]{2,1,0:T(2,128)(2,1)} %copy.99), calls=%async_computation.2 | async-start | bytes 917504 | tf_op jit(solution)/shard_map/all_to_all | solution.py:178
  395.9 8.3 %all-to-all-done.1 = bf16[16,2,7168]{2,1,0:T(2,128)(2,1)S(1)} async-done(((bf16[16,2,7168]{2,1,0:T(2,128)(2,1)}), bf16[16,2,7168]{2,1,0:T(2,128)(2,1)S(1)}, u32[]{:S(2)}, u32[]{:S(2)}) %all-to-all-start.1) | async-done | bytes 458784 | tf_op jit(solution)/shard_map/all_to_all | solution.py:178
  404.2 0.2 reshape.233
  404.4 1.9 fusion
  (82 shorter events, 1.6 us)
Async XLA Ops:
  6.5 306.9 %copy-start = (bf16[1,128,7168]{2,1,0:T(8,128)(2,1)S(1)}, bf16[1,128,7168]{2,1,0:T(8,128)(2,1)}, u32[]{:S(2)}) copy-start(bf16[1,128,7168]{2,1,0:T(8,128)(2,1)} %param.25) | copy-start | bytes 5505028
  6.5 35.1 %copy-start.2 = (bf16[128,512]{1,0:T(8,128)(2,1)S(1)}, bf16[128,512]{1,0:T(8,128)(2,1)}, u32[]{:S(2)}) copy-start(bf16[128,512]{1,0:T(8,128)(2,1)} %param.14) | copy-start | bytes 393220
  6.5 30.8 %copy-start.4 = (bf16[128,512]{1,0:T(8,128)(2,1)S(1)}, bf16[128,512]{1,0:T(8,128)(2,1)}, u32[]{:S(2)}) copy-start(bf16[128,512]{1,0:T(8,128)(2,1)} %param.15) | copy-start | bytes 393220
  6.5 30.7 %copy-start.5 = (bf16[128,512]{1,0:T(8,128)(2,1)S(1)}, bf16[128,512]{1,0:T(8,128)(2,1)}, u32[]{:S(2)}) copy-start(bf16[128,512]{1,0:T(8,128)(2,1)} %param.13) | copy-start | bytes 393220
  6.5 98.1 %all-gather.3.cloned.1.call-start = ((), (), s32[]{:S(2)}) async-start(), calls=%async_computation.3 | async-start | bytes 7798784 | tf_op jit(solution)/shard_map/all_gather | solution.py:138
  7.3 214.9 %all-reduce.3.cloned.1.call-start = ((), (), s32[]{:S(2)}) async-start(), calls=%async_computation.6 | async-start | bytes 7340032
  8.4 71.3 %collective-permute-start.6 = (bf16[128,512]{0,1:T(8,128)(2,1)S(1)}, bf16[128,512]{0,1:T(8,128)(2,1)S(1)}, u32[]{:S(2)}, u32[]{:S(2)}) collective-permute-start(bf16[128,512]{0,1:T(8,128)(2,1)S(1)} %fusion.24), channel_id=1, source_target_pairs={{0,64},{16,80},{32,96},{48,112},{64,128},{80,144},{96,160},{112,17... | collective-permute-start | bytes 393224 | tf_op jit(solution)/shard_map/ppermute | solution.py:15
  13.6 66.2 %collective-permute-start.7 = (bf16[128,512]{0,1:T(8,128)(2,1)S(1)}, bf16[128,512]{0,1:T(8,128)(2,1)S(1)}, u32[]{:S(2)}, u32[]{:S(2)}) collective-permute-start(bf16[128,512]{0,1:T(8,128)(2,1)S(1)} %fusion.24), channel_id=1, source_target_pairs={{0,48},{16,64},{32,80},{48,96},{64,112},{80,128},{96,144},{112,160... | collective-permute-start | bytes 393224 | tf_op jit(solution)/shard_map/ppermute | solution.py:15
  16.6 82.7 %collective-permute-start.8 = (bf16[128,512]{0,1:T(8,128)(2,1)S(1)}, bf16[128,512]{0,1:T(8,128)(2,1)S(1)}, u32[]{:S(2)}, u32[]{:S(2)}) collective-permute-start(bf16[128,512]{0,1:T(8,128)(2,1)S(1)} %fusion.24), channel_id=1, source_target_pairs={{0,32},{16,48},{32,64},{48,80},{64,96},{80,112},{96,128},{112,144}... | collective-permute-start | bytes 393224 | tf_op jit(solution)/shard_map/ppermute | solution.py:15
  21.7 39.6 %collective-permute-start.2 = (bf16[128,512]{1,0:T(8,128)(2,1)}, bf16[128,512]{1,0:T(8,128)(2,1)S(1)}, u32[]{:S(2)}, u32[]{:S(2)}) collective-permute-start(bf16[128,512]{1,0:T(8,128)(2,1)} %param.15), channel_id=1, source_target_pairs={{0,64},{16,80},{32,96},{48,112},{64,128},{80,144},{96,160},{112,17... | collective-permute-start | bytes 393224 | tf_op jit(solution)/shard_map/ppermute | solution.py:15
  26.4 11.6 %collective-permute-start.1 = (bf16[16,512]{1,0:T(8,128)(2,1)}, bf16[16,512]{1,0:T(8,128)(2,1)S(1)}, u32[]{:S(2)}, u32[]{:S(2)}) collective-permute-start(bf16[16,512]{1,0:T(8,128)(2,1)} %slice.74), channel_id=1, source_target_pairs={{16,0},{32,16},{48,32},{64,48},{80,64},{96,80},{112,96},{128,112},... | collective-permute-start | bytes 49160 | tf_op jit(solution)/shard_map/ppermute | solution.py:15
  37.3 24.0 %copy-start.6 = (bf16[16,4,8,128]{3,2,1,0:T(8,128)(2,1)}, bf16[16,4,8,128]{3,2,1,0:T(8,128)(2,1)S(1)}, u32[]{:S(2)}) copy-start(bf16[16,4,8,128]{3,2,1,0:T(8,128)(2,1)S(1)} %fusion.25) | copy-start | bytes 393220
  38.0 26.2 %collective-permute-start.3 = (bf16[128,512]{1,0:T(8,128)(2,1)S(1)}, bf16[128,512]{1,0:T(8,128)(2,1)S(1)}, u32[]{:S(2)}, u32[]{:S(2)}) collective-permute-start(bf16[128,512]{1,0:T(8,128)(2,1)S(1)} %copy-done.4), channel_id=1, source_target_pairs={{0,48},{16,64},{32,80},{48,96},{64,112},{80,128},{96,144},{112,160... | collective-permute-start | bytes 393224 | tf_op jit(solution)/shard_map/ppermute | solution.py:15
  61.3 42.7 %copy-start.10 = (f32[128,4]{0,1:T(4,128)S(1)}, f32[128,4]{0,1:T(4,128)}, u32[]{:S(2)}) copy-start(f32[128,4]{0,1:T(4,128)} %get-tuple-element.8) | copy-start | bytes 6148
  61.3 9.5 %collective-permute-start.4 = (bf16[128,512]{1,0:T(8,128)(2,1)S(1)}, bf16[128,512]{1,0:T(8,128)(2,1)S(1)}, u32[]{:S(2)}, u32[]{:S(2)}) collective-permute-start(bf16[128,512]{1,0:T(8,128)(2,1)S(1)} %copy-done.4), channel_id=1, source_target_pairs={{0,32},{16,48},{32,64},{48,80},{64,96},{80,112},{96,128},{112,144}... | collective-permute-start | bytes 393224 | tf_op jit(solution)/shard_map/ppermute | solution.py:15
  64.2 8.5 %collective-permute-start.5 = (bf16[128,512]{1,0:T(8,128)(2,1)S(1)}, bf16[128,512]{1,0:T(8,128)(2,1)S(1)}, u32[]{:S(2)}, u32[]{:S(2)}) collective-permute-start(bf16[128,512]{1,0:T(8,128)(2,1)S(1)} %copy-done.4), channel_id=1, source_target_pairs={{0,16},{16,32},{32,48},{48,64},{64,80},{80,96},{96,112},{112,128},... | collective-permute-start | bytes 393224 | tf_op jit(solution)/shard_map/ppermute | solution.py:15
  70.8 29.3 %collective-permute-start.9 = (bf16[128,512]{0,1:T(8,128)(2,1)S(1)}, bf16[128,512]{0,1:T(8,128)(2,1)}, u32[]{:S(2)}, u32[]{:S(2)}) collective-permute-start(bf16[128,512]{0,1:T(8,128)(2,1)S(1)} %fusion.24), channel_id=1, source_target_pairs={{0,16},{16,32},{32,48},{48,64},{64,80},{80,96},{96,112},{112,128},... | collective-permute-start | bytes 393224 | tf_op jit(solution)/shard_map/ppermute | solution.py:15
  72.7 5.4 %collective-permute-start = (bf16[16,512]{1,0:T(8,128)(2,1)}, bf16[16,512]{1,0:T(8,128)(2,1)S(1)}, u32[]{:S(2)}, u32[]{:S(2)}) collective-permute-start(bf16[16,512]{1,0:T(8,128)(2,1)} %slice.66), channel_id=1, source_target_pairs={{16,0},{32,16},{48,32},{64,48},{80,64},{96,80},{112,96},{128,112},... | collective-permute-start | bytes 49160 | tf_op jit(solution)/shard_map/ppermute | solution.py:15
  79.8 24.6 %copy-start.9 = (f32[128,4]{0,1:T(4,128)S(1)}, f32[128,4]{0,1:T(4,128)}, u32[]{:S(2)}) copy-start(f32[128,4]{0,1:T(4,128)} %get-tuple-element.7) | copy-start | bytes 6148
  79.8 19.1 %copy-start.8 = (bf16[640,512]{0,1:T(8,128)(2,1)}, bf16[640,512]{0,1:T(8,128)(2,1)S(1)}, u32[]{:S(2)}) copy-start(bf16[640,512]{0,1:T(8,128)(2,1)S(1)} %constant_dynamic-update-slice_fusion.8) | copy-start | bytes 1966084
  99.2 5.2 %copy-start.15 = (bf16[4,128,128]{1,2,0:T(8,128)(2,1)S(1)}, bf16[4,128,128]{1,2,0:T(8,128)(2,1)}, u32[]{:S(2)}) copy-start(bf16[4,128,128]{1,2,0:T(8,128)(2,1)} %get-tuple-element.16) | copy-start | bytes 393220
  112.1 0.7 copy-start.11
  112.1 1.3 copy-start.14
  112.1 110.0 %copy-start.3 = (bf16[8,7168]{1,0:T(8,128)(2,1)S(1)}, bf16[8,7168]{1,0:T(8,128)(2,1)}, u32[]{:S(2)}) copy-start(bf16[8,7168]{1,0:T(8,128)(2,1)} %param.19) | copy-start | bytes 344068
  112.1 111.1 %copy-start.7 = (f32[7168]{0:T(1024)S(1)}, f32[7168]{0:T(1024)}, u32[]{:S(2)}) copy-start(f32[7168]{0:T(1024)} %param.20) | copy-start | bytes 86020
  112.2 177.6 %all-gather.5.cloned.1.call-start = ((), (), s32[]{:S(2)}) async-start(), calls=%async_computation.4 | async-start | bytes 7798784 | tf_op jit(solution)/shard_map/all_gather | solution.py:167
  239.8 146.4 %reduce-scatter.2.cloned.1.call-start = ((), (), s32[]{:S(2)}) async-start(), calls=%async_computation.5 | async-start | bytes 7798784 | tf_op jit(solution)/shard_map/reduce_scatter | solution.py:175
  305.2 5.8 %copy-start.1 = (bf16[512,7168]{1,0:T(8,128)(2,1)S(1)}, bf16[512,7168]{1,0:T(8,128)(2,1)}, u32[]{:S(2)}) copy-start(bf16[512,7168]{1,0:T(8,128)(2,1)} %reshape.232) | copy-start | bytes 22020100
  305.2 6.2 %copy-start.13 = (bf16[1,7168,128]{2,1,0:T(8,128)(2,1)S(1)}, bf16[1,7168,128]{2,1,0:T(8,128)(2,1)}, u32[]{:S(2)}) copy-start(bf16[1,7168,128]{2,1,0:T(8,128)(2,1)} %param.24) | copy-start | bytes 5505028
  318.4 77.4 %copy-start.12 = (f32[8,2]{0,1:T(2,128)S(1)}, f32[8,2]{0,1:T(2,128)}, u32[]{:S(2)}) copy-start(f32[8,2]{0,1:T(2,128)} %param.22) | copy-start | bytes 196
  388.6 15.6 %all-to-all-start.1 = ((bf16[16,2,7168]{2,1,0:T(2,128)(2,1)}), bf16[16,2,7168]{2,1,0:T(2,128)(2,1)S(1)}, u32[]{:S(2)}, u32[]{:S(2)}) async-start(bf16[16,2,7168]{2,1,0:T(2,128)(2,1)} %copy.99), calls=%async_computation.2 | async-start | bytes 917504 | tf_op jit(solution)/shard_map/all_to_all | solution.py:178
Sparse Core Ops, SparseCore 0:
  9.2 68.1 all-gather.2
  112.3 109.8 all-reduce.2
  240.0 49.7 all-gather.4
  318.6 67.6 reduce-scatter.1
where the time goes:
time: 414 us; the launch traced here: 413 us
  waiting for transfers between devices  243 us (59%)
  blocking collectives  52.3 us (13%)
  starting transfers between devices  37.2 us (9%)
  local copies, waits for them, and re-layouts  31.5 us (8%)
  matrix products  29.6 us (7%)
  between operations  14.3 us (3%)
  other arithmetic  5.39 us (1%)
    unnamed x5, waiting for transfers between devices  108 us
    reduce_scatter x1, waiting for transfers between devices, local(): lax.psum_scatter(partial_out.astype(jnp.bfloat16), 'ctx', scatter_dimensi...  67.8 us
    all_gather x1, waiting for transfers between devices, local(): portion = lax.all_gather(arrived, 'ctx', axis=0, tiled=True)  49.7 us
    ppermute x10, starting transfers between devices, passed_along(): return lax.ppermute(block, axis, route)  29.6 us
    all_gather x1, blocking collectives, local(): part_values = lax.all_gather(comp_values, 'ctx', axis=0, tiled=True)  19 us
    all_gather x1, blocking collectives, local(): part_keys = lax.all_gather(comp_keys, 'ctx', axis=0, tiled=True)  18.2 us
    reshape x1, local copies, waits for them, and re-layouts, local(): flat_rows = portion.reshape(-1, model_width)  15.4 us
    all_to_all x1, blocking collectives, local(): lax.all_to_all(outgoing, 'exp', split_axis=0, concat_axis=0, tiled=True)  15.1 us
  transfers between devices with their start and end apart: 15, of which 6 were waited for; matrix products, arithmetic and copies ran while one was open for 6% of the time, Pallas kernels for 0%

commit v1 on v0

--- a/solution.py
+++ b/solution.py
@@ -164,7 +164,9 @@
     gate_cols = expert_gate[0]
     up_cols = expert_up[0]
     down_rows = expert_down[0]
-    portion = lax.all_gather(arrived, "ctx", axis=0, tiled=True)
+    portion = jnp.concatenate(
+        lax.all_to_all(jnp.stack([arrived] * lax.axis_size("ctx")), "ctx", 0, 0), axis=0
+    )
     flat_rows = portion.reshape(-1, model_width)
     gate_part = jnp.dot(flat_rows, gate_cols, preferred_element_type=jnp.float32)
     up_part = jnp.dot(flat_rows, up_cols, preferred_element_type=jnp.float32)

time: 414 us -> 537 us (1.30)
  blocking collectives: 52.3 us -> 221 us
  waiting for transfers between devices: 243 us -> 190 us
  local copies, waits for them, and re-layouts: 31.5 us -> 37.8 us
    all_to_all x0 -> x1, blocking collectives: none -> 169 us  [local(): lax.all_to_all(jnp.stack([arrived] * lax.axis_size('ctx')), 'ctx', 0, 0)]
    all_gather x1 -> x0, waiting for transfers between devices: 49.7 us -> none  [local(): portion = lax.all_gather(arrived, 'ctx', axis=0, tiled=True)]
    another operation x0 -> x2, local copies, waits for them, and re-layouts: none -> 21.7 us  [the longest x1 15.4 us: local(): flat_rows = portion.reshape(-1, model_width)]
    reshape x1 -> x0, local copies, waits for them, and re-layouts: 15.4 us -> none  [local(): flat_rows = portion.reshape(-1, model_width)]
    unnamed x5 -> x4, waiting for transfers between devices: 108 us -> 108 us
  transfers between devices with their start and end apart: 15 -> 14, of which waited for: 6 -> 5; matrix products, arithmetic and copies ran while one was open for 6% -> 4% of each run, Pallas kernels for 0% -> 0%
where the time goes in v1:
time: 537 us; the launch traced here: 535 us
  blocking collectives  221 us (41%)
  waiting for transfers between devices  190 us (35%)
  local copies, waits for them, and re-layouts  37.8 us (7%)
  starting transfers between devices  37 us (7%)
  matrix products  29.6 us (6%)
  between operations  14.3 us (3%)
  other arithmetic  5.38 us (1%)
    all_to_all x1, blocking collectives, local(): lax.all_to_all(jnp.stack([arrived] * lax.axis_size('ctx')), 'ctx', 0, 0)  169 us
    unnamed x4, waiting for transfers between devices  108 us
    reduce_scatter x1, waiting for transfers between devices, local(): lax.psum_scatter(partial_out.astype(jnp.bfloat16), 'ctx', scatter_dimensi...  65.1 us
    ppermute x10, starting transfers between devices, passed_along(): return lax.ppermute(block, axis, route)  29.6 us
    all_gather x1, blocking collectives, local(): part_values = lax.all_gather(comp_values, 'ctx', axis=0, tiled=True)  19.1 us
    all_gather x1, blocking collectives, local(): part_keys = lax.all_gather(comp_keys, 'ctx', axis=0, tiled=True)  18.2 us
    another operation x1, local copies, waits for them, and re-layouts, local(): flat_rows = portion.reshape(-1, model_width)  15.4 us
    all_to_all x1, blocking collectives, local(): lax.all_to_all(outgoing, 'exp', split_axis=0, concat_axis=0, tiled=True)  15 us
  transfers between devices with their start and end apart: 14, of which 5 were waited for; matrix products, arithmetic and copies ran while one was open for 4% of the time, Pallas kernels for 0%

profile of v1, /device:TPU:8, one launch (start us, length us, event | category | flops | bytes accessed | tf_op | source)
XLA Modules:
  0.0 535.4 jit_solution(12682539696160982535)
XLA Ops:
  6.6 0.7 all-gather.2.cloned.1.call-update
  7.3 1.0 copy.91
  8.4 5.2 collective-permute-start.6
  13.6 3.0 collective-permute-start.7
  16.6 5.0 collective-permute-start.8
  21.7 3.4 collective-permute-start.2
  25.1 1.3 slice.74
  26.4 1.3 collective-permute-start.1
  27.7 1.6 slice.71
  29.3 0.9 slice.63
  30.2 0.9 convert_multiply_fusion.3
  31.3 0.2 reduce_sum.83
  31.5 0.7 add_divide_fusion
  32.2 0.6 slice_bitcast_fusion.1
  32.8 1.4 fusion.49
  34.3 0.8 and_and_fusion
  35.1 1.1 fusion.30
  36.3 0.8 fusion.34
  37.1 0.2 mul.134
  37.3 0.7 slice.66
  38.0 3.6 collective-permute-start.3
  41.7 0.2 fusion.28
  42.1 18.2 %all_gather.10 = bf16[128,512]{1,0:T(8,128)(2,1)S(1)} all-gather(bf16[8,512]{1,0:T(8,128)(2,1)S(1)} %fusion.45), channel_id=1, replica_groups=mesh['ctx'=16,'exp'=16] {'ctx'}, dimensions={0}, use_global_device_ids=true | all-gather | bytes 139264 | tf_op jit(solution)/shard_map/all_gather | solution.py:74
  60.3 0.1 copy.86
  60.4 0.9 fusion.51
  61.4 2.9 collective-permute-start.4
  64.3 2.0 collective-permute-start.5
  66.3 4.4 collective-permute-done.4
  70.7 2.0 collective-permute-start.9
  72.7 1.3 collective-permute-start
  74.0 4.0 collective-permute-done
  78.1 0.9 fusion.32
  79.0 0.7 fusion.44
  79.8 19.1 %all_gather.9 = bf16[128,512]{1,0:T(8,128)(2,1)S(1)} all-gather(bf16[8,512]{1,0:T(8,128)(2,1)S(1)} %fusion.44), channel_id=1, replica_groups=mesh['ctx'=16,'exp'=16] {'ctx'}, dimensions={0}, use_global_device_ids=true | all-gather | bytes 139264 | tf_op jit(solution)/shard_map/all_gather | solution.py:75
  98.9 0.3 copy.90
  99.2 0.1 copy.83
  99.4 0.7 constant_dynamic-update-slice_fusion.7
  100.1 1.6 constant_dynamic-update-slice_fusion.6
  101.6 0.7 constant_dynamic-update-slice_fusion.5
  102.3 1.7 fusion.50
  104.0 0.4 fusion.17
  104.4 0.2 fusion.18
  104.6 7.5 %fusion.52 = f32[128,7168]{1,0:T(8,128)} fusion(bf16[128,512]{0,1:T(8,128)(2,1)S(1)} %bitcast.126, bf16[512,7168]{0,1:T(8,128)(2,1)} %all-gather.2.cloned.1.call-done), kind=kOutput, calls=%fused_computation.101 | convolution fusion | flops 939524096 | bytes 11141120 | tf_op jit(solution)/shard_map/dot_general | solution.py:136
  112.2 0.6 copy-done.11
  113.1 0.2 select_reduce_fusion.1
  113.4 0.6 dynamic-slice
  114.7 107.4 %all-reduce.3.cloned.1.call-done = f32[128,7168]{1,0:T(8,128)} async-done(((f32[128,7168]{1,0:T(8,128)}), f32[128,7168]{1,0:T(8,128)}) %all-reduce.3.cloned.1.call-update) | async-done | bytes 3670032
  222.1 1.1 multiply_reduce_fusion
  223.3 1.3 convolution_convert_fusion.1
  224.6 0.2 reshape.230
  224.7 15.0 %all_to_all.15 = bf16[16,2,7168]{2,1,0:T(2,128)(2,1)S(1)} all-to-all(bf16[16,2,7168]{2,1,0:T(2,128)(2,1)S(1)} %reshape.230), channel_id=1, replica_groups=mesh['ctx'=16,'exp'=16] {'exp'}, dimensions={0} | all-to-all | bytes 917504 | tf_op jit(solution)/shard_map/all_to_all | solution.py:163
  239.7 6.3 %stack.2 = bf16[16,16,2,7168]{3,2,1,0:T(2,128)(2,1)S(1)} broadcast(bf16[16,2,7168]{2,1,0:T(2,128)(2,1)S(1)} %all_to_all.15), dimensions={1,2,3} | broadcast | bytes 7798784 | tf_op jit(solution)/shard_map/stack | solution.py:168
  246.0 169.0 %all_to_all.16 = bf16[16,16,2,7168]{3,2,1,0:T(2,128)(2,1)} all-to-all(bf16[16,16,2,7168]{3,2,1,0:T(2,128)(2,1)S(1)} %stack.2), channel_id=1, replica_groups=mesh['ctx'=16,'exp'=16] {'ctx'}, dimensions={0} | all-to-all | bytes 14680064 | tf_op jit(solution)/shard_map/all_to_all | solution.py:168
  415.0 15.4 %reshape_reshape.3 = bf16[512,7168]{1,0:T(8,128)(2,1)} reshape(bf16[16,16,2,7168]{3,2,1,0:T(2,128)(2,1)} %all_to_all.16) | data formatting | bytes 14680064 | tf_op jit(solution)/shard_map/reshape;reshape | solution.py:170
  430.5 5.8 %fusion.4 = f32[512,128]{1,0:T(8,128)S(1)} fusion(bf16[512,7168]{1,0:T(8,128)(2,1)} %reshape_reshape.3, bf16[1,7168,128]{2,1,0:T(8,128)(2,1)} %param.23), kind=kOutput, calls=%fused_computation.7 | convolution fusion | flops 939524096 | bytes 9437184 | tf_op jit(solution)/shard_map/dot_general | solution.py:171
  436.3 0.4 copy-done.13
  436.7 2.1 fusion.19
  438.7 5.0 convolution_convert_fusion
  443.8 65.1 %reduce-scatter.2.cloned.1.call-done = bf16[16,2,7168]{2,0,1:T(8,128)(2,1)} async-done(((bf16[256,2,7168]{2,0,1:T(8,128)(2,1)}), bf16[16,2,7168]{2,0,1:T(8,128)(2,1)}) %reduce-scatter.2.cloned.1.call-update) | async-done | bytes 458768 | tf_op jit(solution)/shard_map/reduce_scatter | solution.py:177
  508.8 2.3 copy.99
  511.1 7.3 %all-to-all-start.2 = ((bf16[16,2,7168]{2,1,0:T(2,128)(2,1)}), bf16[16,2,7168]{2,1,0:T(2,128)(2,1)S(1)}, u32[]{:S(2)}, u32[]{:S(2)}) async-start(bf16[16,2,7168]{2,1,0:T(2,128)(2,1)} %copy.99), calls=%async_computation.3 | async-start | bytes 917504 | tf_op jit(solution)/shard_map/all_to_all | solution.py:180
  518.5 8.3 %all-to-all-done.2 = bf16[16,2,7168]{2,1,0:T(2,128)(2,1)S(1)} async-done(((bf16[16,2,7168]{2,1,0:T(2,128)(2,1)}), bf16[16,2,7168]{2,1,0:T(2,128)(2,1)S(1)}, u32[]{:S(2)}, u32[]{:S(2)}) %all-to-all-start.2) | async-done | bytes 458784 | tf_op jit(solution)/shard_map/all_to_all | solution.py:180
  526.8 0.2 reshape.231
  526.9 1.9 fusion
  (81 shorter events, 1.6 us)
Async XLA Ops:
  6.5 432.2 %copy-start = (bf16[1,128,7168]{2,1,0:T(8,128)(2,1)S(1)}, bf16[1,128,7168]{2,1,0:T(8,128)(2,1)}, u32[]{:S(2)}) copy-start(bf16[1,128,7168]{2,1,0:T(8,128)(2,1)} %param.25) | copy-start | bytes 5505028
  6.5 35.1 %copy-start.2 = (bf16[128,512]{1,0:T(8,128)(2,1)S(1)}, bf16[128,512]{1,0:T(8,128)(2,1)}, u32[]{:S(2)}) copy-start(bf16[128,512]{1,0:T(8,128)(2,1)} %param.14) | copy-start | bytes 393220
  6.5 30.8 %copy-start.4 = (bf16[128,512]{1,0:T(8,128)(2,1)S(1)}, bf16[128,512]{1,0:T(8,128)(2,1)}, u32[]{:S(2)}) copy-start(bf16[128,512]{1,0:T(8,128)(2,1)} %param.15) | copy-start | bytes 393220
  6.5 30.7 %copy-start.5 = (bf16[128,512]{1,0:T(8,128)(2,1)S(1)}, bf16[128,512]{1,0:T(8,128)(2,1)}, u32[]{:S(2)}) copy-start(bf16[128,512]{1,0:T(8,128)(2,1)} %param.13) | copy-start | bytes 393220
  6.5 98.0 %all-gather.2.cloned.1.call-start = ((), (), s32[]{:S(2)}) async-start(), calls=%async_computation.4 | async-start | bytes 7798784 | tf_op jit(solution)/shard_map/all_gather | solution.py:138
  7.3 214.9 %all-reduce.3.cloned.1.call-start = ((), (), s32[]{:S(2)}) async-start(), calls=%async_computation.6 | async-start | bytes 7340032
  8.4 71.2 %collective-permute-start.6 = (bf16[128,512]{0,1:T(8,128)(2,1)S(1)}, bf16[128,512]{0,1:T(8,128)(2,1)S(1)}, u32[]{:S(2)}, u32[]{:S(2)}) collective-permute-start(bf16[128,512]{0,1:T(8,128)(2,1)S(1)} %fusion.24), channel_id=1, source_target_pairs={{0,64},{16,80},{32,96},{48,112},{64,128},{80,144},{96,160},{112,17... | collective-permute-start | bytes 393224 | tf_op jit(solution)/shard_map/ppermute | solution.py:15
  13.6 66.1 %collective-permute-start.7 = (bf16[128,512]{0,1:T(8,128)(2,1)S(1)}, bf16[128,512]{0,1:T(8,128)(2,1)S(1)}, u32[]{:S(2)}, u32[]{:S(2)}) collective-permute-start(bf16[128,512]{0,1:T(8,128)(2,1)S(1)} %fusion.24), channel_id=1, source_target_pairs={{0,48},{16,64},{32,80},{48,96},{64,112},{80,128},{96,144},{112,160... | collective-permute-start | bytes 393224 | tf_op jit(solution)/shard_map/ppermute | solution.py:15
  16.6 82.7 %collective-permute-start.8 = (bf16[128,512]{0,1:T(8,128)(2,1)S(1)}, bf16[128,512]{0,1:T(8,128)(2,1)S(1)}, u32[]{:S(2)}, u32[]{:S(2)}) collective-permute-start(bf16[128,512]{0,1:T(8,128)(2,1)S(1)} %fusion.24), channel_id=1, source_target_pairs={{0,32},{16,48},{32,64},{48,80},{64,96},{80,112},{96,128},{112,144}... | collective-permute-start | bytes 393224 | tf_op jit(solution)/shard_map/ppermute | solution.py:15
  21.7 39.7 %collective-permute-start.2 = (bf16[128,512]{1,0:T(8,128)(2,1)}, bf16[128,512]{1,0:T(8,128)(2,1)S(1)}, u32[]{:S(2)}, u32[]{:S(2)}) collective-permute-start(bf16[128,512]{1,0:T(8,128)(2,1)} %param.15), channel_id=1, source_target_pairs={{0,64},{16,80},{32,96},{48,112},{64,128},{80,144},{96,160},{112,17... | collective-permute-start | bytes 393224 | tf_op jit(solution)/shard_map/ppermute | solution.py:15
  26.4 11.6 %collective-permute-start.1 = (bf16[16,512]{1,0:T(8,128)(2,1)}, bf16[16,512]{1,0:T(8,128)(2,1)S(1)}, u32[]{:S(2)}, u32[]{:S(2)}) collective-permute-start(bf16[16,512]{1,0:T(8,128)(2,1)} %slice.74), channel_id=1, source_target_pairs={{16,0},{32,16},{48,32},{64,48},{80,64},{96,80},{112,96},{128,112},... | collective-permute-start | bytes 49160 | tf_op jit(solution)/shard_map/ppermute | solution.py:15
  37.3 24.0 %copy-start.6 = (bf16[16,4,8,128]{3,2,1,0:T(8,128)(2,1)}, bf16[16,4,8,128]{3,2,1,0:T(8,128)(2,1)S(1)}, u32[]{:S(2)}) copy-start(bf16[16,4,8,128]{3,2,1,0:T(8,128)(2,1)S(1)} %fusion.25) | copy-start | bytes 393220
  38.0 26.3 %collective-permute-start.3 = (bf16[128,512]{1,0:T(8,128)(2,1)S(1)}, bf16[128,512]{1,0:T(8,128)(2,1)S(1)}, u32[]{:S(2)}, u32[]{:S(2)}) collective-permute-start(bf16[128,512]{1,0:T(8,128)(2,1)S(1)} %copy-done.4), channel_id=1, source_target_pairs={{0,48},{16,64},{32,80},{48,96},{64,112},{80,128},{96,144},{112,160... | collective-permute-start | bytes 393224 | tf_op jit(solution)/shard_map/ppermute | solution.py:15
  61.3 42.6 %copy-start.10 = (f32[128,4]{0,1:T(4,128)S(1)}, f32[128,4]{0,1:T(4,128)}, u32[]{:S(2)}) copy-start(f32[128,4]{0,1:T(4,128)} %get-tuple-element.8) | copy-start | bytes 6148
  61.4 9.4 %collective-permute-start.4 = (bf16[128,512]{1,0:T(8,128)(2,1)S(1)}, bf16[128,512]{1,0:T(8,128)(2,1)S(1)}, u32[]{:S(2)}, u32[]{:S(2)}) collective-permute-start(bf16[128,512]{1,0:T(8,128)(2,1)S(1)} %copy-done.4), channel_id=1, source_target_pairs={{0,32},{16,48},{32,64},{48,80},{64,96},{80,112},{96,128},{112,144}... | collective-permute-start | bytes 393224 | tf_op jit(solution)/shard_map/ppermute | solution.py:15
  64.3 8.4 %collective-permute-start.5 = (bf16[128,512]{1,0:T(8,128)(2,1)S(1)}, bf16[128,512]{1,0:T(8,128)(2,1)S(1)}, u32[]{:S(2)}, u32[]{:S(2)}) collective-permute-start(bf16[128,512]{1,0:T(8,128)(2,1)S(1)} %copy-done.4), channel_id=1, source_target_pairs={{0,16},{16,32},{32,48},{48,64},{64,80},{80,96},{96,112},{112,128},... | collective-permute-start | bytes 393224 | tf_op jit(solution)/shard_map/ppermute | solution.py:15
  70.7 29.3 %collective-permute-start.9 = (bf16[128,512]{0,1:T(8,128)(2,1)S(1)}, bf16[128,512]{0,1:T(8,128)(2,1)}, u32[]{:S(2)}, u32[]{:S(2)}) collective-permute-start(bf16[128,512]{0,1:T(8,128)(2,1)S(1)} %fusion.24), channel_id=1, source_target_pairs={{0,16},{16,32},{32,48},{48,64},{64,80},{80,96},{96,112},{112,128},... | collective-permute-start | bytes 393224 | tf_op jit(solution)/shard_map/ppermute | solution.py:15
  72.7 5.3 collective-permute-start
  79.7 24.6 %copy-start.9 = (f32[128,4]{0,1:T(4,128)S(1)}, f32[128,4]{0,1:T(4,128)}, u32[]{:S(2)}) copy-start(f32[128,4]{0,1:T(4,128)} %get-tuple-element.7) | copy-start | bytes 6148
  79.8 19.1 %copy-start.8 = (bf16[640,512]{0,1:T(8,128)(2,1)}, bf16[640,512]{0,1:T(8,128)(2,1)S(1)}, u32[]{:S(2)}) copy-start(bf16[640,512]{0,1:T(8,128)(2,1)S(1)} %constant_dynamic-update-slice_fusion.8) | copy-start | bytes 1966084
  99.2 5.1 copy-start.15
  112.1 0.7 copy-start.11
  112.1 1.3 copy-start.14
  112.1 110.0 %copy-start.3 = (bf16[8,7168]{1,0:T(8,128)(2,1)S(1)}, bf16[8,7168]{1,0:T(8,128)(2,1)}, u32[]{:S(2)}) copy-start(bf16[8,7168]{1,0:T(8,128)(2,1)} %param.19) | copy-start | bytes 344068
  112.1 111.2 %copy-start.7 = (f32[7168]{0:T(1024)S(1)}, f32[7168]{0:T(1024)}, u32[]{:S(2)}) copy-start(f32[7168]{0:T(1024)} %param.20) | copy-start | bytes 86020
  112.1 396.7 %reduce-scatter.2.cloned.1.call-start = ((), (), s32[]{:S(2)}) async-start(), calls=%async_computation.5 | async-start | bytes 7798784 | tf_op jit(solution)/shard_map/reduce_scatter | solution.py:177
  430.5 5.8 %copy-start.1 = (bf16[512,7168]{1,0:T(8,128)(2,1)S(1)}, bf16[512,7168]{1,0:T(8,128)(2,1)}, u32[]{:S(2)}) copy-start(bf16[512,7168]{1,0:T(8,128)(2,1)} %reshape_reshape.3) | copy-start | bytes 22020100
  430.5 6.2 %copy-start.13 = (bf16[1,7168,128]{2,1,0:T(8,128)(2,1)S(1)}, bf16[1,7168,128]{2,1,0:T(8,128)(2,1)}, u32[]{:S(2)}) copy-start(bf16[1,7168,128]{2,1,0:T(8,128)(2,1)} %param.24) | copy-start | bytes 5505028
  443.8 74.6 %copy-start.12 = (f32[8,2]{0,1:T(2,128)S(1)}, f32[8,2]{0,1:T(2,128)}, u32[]{:S(2)}) copy-start(f32[8,2]{0,1:T(2,128)} %param.22) | copy-start | bytes 196
  511.1 15.6 %all-to-all-start.2 = ((bf16[16,2,7168]{2,1,0:T(2,128)(2,1)}), bf16[16,2,7168]{2,1,0:T(2,128)(2,1)S(1)}, u32[]{:S(2)}, u32[]{:S(2)}) async-start(bf16[16,2,7168]{2,1,0:T(2,128)(2,1)} %copy.99), calls=%async_computation.3 | async-start | bytes 917504 | tf_op jit(solution)/shard_map/all_to_all | solution.py:180
Sparse Core Ops, SparseCore 0:
  9.2 68.1 all-gather.1
  112.3 109.8 all-reduce.2
  443.9 64.8 reduce-scatter.1
